TPU v7x, 512 devices: a whole 4x4x16 slice. The times are simulated.
512 devices in a mesh: row: 128 (over x, z_hi, y, core), col: 4 (over z_lo).
Axes of the slice: x: 4, y: 4, z: 16 (z_hi: 4, z_lo: 4; z = z_hi * 4 + z_lo), core: 2. Of those that a mesh axis runs over, the one named last changes fastest.
Arguments:
- diag_inverse: float32 [512, 512], replicated, may hold values from -1 to 2, as said below
- panel: float32 [12288, 512], P('row', 'col'), may hold values from -0.3 to 0.3
- trailing: float32 [12288, 12288], P('row', 'col'), may hold values from -6 to 6
- agg_vals: float32 [128, 4, 192, 1024], P('row', 'col'), may hold values from -6 to 6
- agg_dest: int32 [128, 4, 192, 1], P('row', 'col'), may hold values from 0 to 127; in each aligned block of 192 rows (0 to 191, 192 to 383, ..., all dimensions but the last counted through in order) at most 2 rows name the same one
- agg_tile: int32 [128, 4, 192], P('row', 'col'), may hold values from 0 to 287
Outputs:
- updated: float32 [12288, 12288], P('row', 'col')
- panel_factor: float32 [12288, 512], P('row', 'col')
Inputs may be any that keep to these rules, and one draw needn't show every extreme that they name: `diag_inverse`: lower triangular with diagonal entries between 0.5 and 2. `agg_dest`: among the aggregates of one device no row index is named more than 2 times, and in some device one is named exactly 2 times.
All inputs are finite; a program needn't handle non-finite values.
Results may differ from a plain program's by a relative error of at most 0.000071.
Values sent between devices are 32-bit elements; how exact they have to be, the bound alone decides.
A program may use at most 64 MiB of HBM per device.

v0:
```python
import jax
import jax.numpy as jnp
from jax import lax
from jax.sharding import PartitionSpec as P

TILE_ROWS = 8
TILE_COLS = 128
CAP = 2


def per_device(diag_inverse, panel, trailing, agg_vals, agg_dest, agg_tile):
    row_devices = lax.axis_size("row")
    col_devices = lax.axis_size("col")
    local_rows, local_cols = trailing.shape
    panel_width = diag_inverse.shape[0]
    part_width = panel_width // col_devices
    col_index = lax.axis_index("col")
    contract_last = (((1,), (1,)), ((), ()))
    panel_whole = lax.all_gather(panel, "col", axis=1, tiled=True)
    own_full = jnp.dot(
        panel_whole,
        diag_inverse.T,
        precision=lax.Precision.HIGHEST,
        preferred_element_type=jnp.float32,
    )
    own_block = lax.dynamic_slice_in_dim(own_full, col_index * part_width, part_width, 1)
    column_all = lax.all_gather(own_block, "row", axis=0, tiled=True)
    split_rows = column_all.reshape(col_devices, local_cols, part_width)
    swapped = lax.all_to_all(split_rows, "col", split_axis=0, concat_axis=2, tiled=True)
    partner = swapped.reshape(local_cols, panel_width)
    tile_rows = local_rows // TILE_ROWS
    tile_cols = local_cols // TILE_COLS
    tiles_dev = tile_rows * tile_cols
    tile_values = agg_vals.reshape(agg_vals.shape[2], agg_vals.shape[3])
    targets = agg_dest.reshape(-1)
    tile_ids = agg_tile.reshape(-1)
    matches = (targets[:, None] == jnp.arange(row_devices, dtype=jnp.int32)[None, :]).astype(
        jnp.int32
    )
    earlier = jnp.cumsum(matches, axis=0) - matches
    ranks = jnp.sum(earlier * matches, axis=1)
    position = targets * CAP + ranks
    send_values = (
        jnp.zeros((row_devices * CAP, tile_values.shape[1]), jnp.float32)
        .at[position]
        .set(tile_values)
    )
    send_ids = (
        jnp.full((row_devices * CAP,), float(tiles_dev), jnp.float32)
        .at[position]
        .set(tile_ids.astype(jnp.float32))
    )
    got_values, got_ids = (
        lax.all_to_all(send_values, "row", split_axis=0, concat_axis=0, tiled=True),
        lax.all_to_all(send_ids, "row", split_axis=0, concat_axis=0, tiled=True),
    )
    landing = got_ids.astype(jnp.int32)
    blocked = trailing.reshape(tile_rows, TILE_ROWS, tile_cols, TILE_COLS)
    blocked = blocked.at[landing // tile_cols, :, landing % tile_cols, :].add(
        got_values.reshape(-1, TILE_ROWS, TILE_COLS), mode="drop"
    )
    assembled = blocked.reshape(local_rows, local_cols)
    product = lax.dot_general(
        own_full,
        partner,
        contract_last,
        precision=lax.Precision.HIGHEST,
        preferred_element_type=jnp.float32,
    )
    updated = assembled - product
    return (updated, own_block)


def solution(mesh):
    in_specs = (
        P(),
        P("row", "col"),
        P("row", "col"),
        P("row", "col", None, None),
        P("row", "col", None, None),
        P("row", "col", None),
    )
    out_specs = (P("row", "col"), P("row", "col"))
    return jax.shard_map(
        per_device, mesh=mesh, in_specs=in_specs, out_specs=out_specs, check_vma=False
    )
```

profile of v0, /device:TPU:1, one launch (start us, length us, event | category | flops | bytes accessed | tf_op | source)
XLA Modules:
  0.0 355.4 jit_solution(15490305446457586598)
XLA Ops:
  7.2 0.0 copy-start
  7.2 0.0 copy-start.4
  7.2 0.0 all-gather.2.cloned.1.call-start
  7.2 0.0 copy-start.5
  7.2 0.8 copy-done.4
  8.1 13.3 %all_gather.6 = f32[96,512]{1,0:T(8,128)S(1)} all-gather(f32[96,128]{1,0:T(8,128)S(1)} %copy-done.4), channel_id=1, replica_groups=mesh['row'=128,'col'=4] {'col'}, dimensions={1}, use_global_device_ids=true | all-gather | bytes 245760 | tf_op jit(solution)/shard_map/all_gather | solution.py:19
  21.3 0.0 copy-done
  21.4 0.0 copy-start.6
  21.4 0.0 copy-start.3
  21.4 1.1 fusion.10
  22.5 0.6 constant_dynamic-slice_fusion
  23.1 0.0 all-gather.2.cloned.1.call-update
  23.2 0.0 copy-done.5
  23.2 0.1 iota_compare_fusion
  23.3 0.1 fusion.3
  23.5 0.0 copy-done.6
  23.5 0.2 fusion.6
  23.7 1.2 scatter_custom_fusion
  24.9 0.8 all_to_all.23
  25.7 23.4 %all-to-all-start = ((f32[128,2,1]{1,2,0:T(1,128)}), f32[128,2,1]{1,2,0:T(1,128)S(1)}, u32[]{:S(2)}, u32[]{:S(2)}) async-start(f32[128,2,1]{1,2,0:T(1,128)} %bitcast.10), calls=%async_computation | async-start | bytes 131072 | tf_op jit(solution)/shard_map/all_to_all | solution.py:55
  49.1 0.0 copy-done.3
  49.1 1.5 scatter_custom_fusion.1
  50.6 1.6 all_to_all.25
  52.2 13.9 %all-to-all-done = f32[128,2,1]{1,2,0:T(1,128)S(1)} async-done(((f32[128,2,1]{1,2,0:T(1,128)}), f32[128,2,1]{1,2,0:T(1,128)S(1)}, u32[]{:S(2)}, u32[]{:S(2)}) %all-to-all-start) | async-done | bytes 1056 | tf_op jit(solution)/shard_map/all_to_all | solution.py:55
  66.1 6.9 %all-to-all-start.1 = ((f32[128,2,1024]{2,1,0:T(2,128)}), f32[128,2,1024]{2,1,0:T(2,128)S(1)}, u32[]{:S(2)}, u32[]{:S(2)}) async-start(f32[128,2,1024]{2,1,0:T(2,128)} %all_to_all.25), calls=%async_computation.1 | async-start | bytes 2097152 | tf_op jit(solution)/shard_map/all_to_all | solution.py:54
  73.0 117.3 %all-gather.2.cloned.1.call-done = f32[12288,128]{1,0:T(8,128)} async-done(((f32[96,128]{1,0:T(8,128)}), f32[12288,128]{1,0:T(8,128)}) %all-gather.2.cloned.1.call-update) | async-done | bytes 6291472 | tf_op jit(solution)/shard_map/all_gather | solution.py:27
  190.3 6.5 %copy.14 = f32[4,3072,128]{1,2,0:T(8,128)} copy(f32[4,3072,128]{2,1,0:T(8,128)} %bitcast.37) | data formatting | bytes 12582912 | tf_op jit(solution)/shard_map/reshape | solution.py:28
  196.8 0.0 all-to-all-done.1
  196.8 0.0 copy-start.2
  196.8 1.0 copy-done.2
  197.8 5.4 %all-to-all-start.2 = ((f32[4,3072,128]{1,2,0:T(8,128)}), f32[4,3072,128]{1,2,0:T(8,128)}, u32[]{:S(2)}, u32[]{:S(2)}) async-start(f32[4,3072,128]{1,2,0:T(8,128)} %copy.14), calls=%async_computation.2 | async-start | bytes 12582912 | tf_op jit(solution)/shard_map/all_to_all | solution.py:29
  203.2 0.5 divide_reduce_fusion
  203.7 0.0 copy-start.1
  203.7 0.1 rem.30
  203.9 0.1 div.17
  204.0 0.3 compare_reduce_fusion
  204.3 0.1 ne.52
  204.5 2.1 reshape.174
  206.6 0.0 copy-done.1
  206.6 11.5 %scatter_fusion = f32[12,8,24,128]{3,1,2,0:T(8,128)S(1)} fusion(f32[12,8,24,128]{3,1,2,0:T(8,128)S(1)} %bitcast.36, s32[256]{0:T(256)S(1)} %bitcast.35, f32[256,8,128]{2,1,0:T(8,128)S(1)} %reshape.174), kind=kCustom, calls=%fused_computation.2 | custom fusion | flops 262144 | bytes 3147776 | tf_op jit(solution)/shard_map/scatter-add | solution.py:59
  218.1 123.0 %all-to-all-done.2 = f32[4,3072,128]{1,2,0:T(8,128)} async-done(((f32[4,3072,128]{1,2,0:T(8,128)}), f32[4,3072,128]{1,2,0:T(8,128)}, u32[]{:S(2)}, u32[]{:S(2)}) %all-to-all-start.2) | async-done | bytes 6291488 | tf_op jit(solution)/shard_map/all_to_all | solution.py:29
  341.1 7.5 %convolution_subtract_fusion = f32[96,3072]{1,0:T(8,128)} fusion(f32[96,512]{1,0:T(8,128)S(1)} %fusion.10, f32[3072,512]{0,1:T(8,128)} %bitcast.17, f32[12,8,24,128]{3,1,2,0:T(8,128)S(1)} %scatter_fusion), kind=kOutput, calls=%fused_computation.3 | convolution fusion | flops 1812234240 | bytes 8847360 | tf_op jit(solution)/shard_map/dot_general | solution.py:63
  (10 shorter events, 0.1 us)
Async XLA Ops:
  7.2 14.2 %copy-start = (f32[512,512]{1,0:T(8,128)S(1)}, f32[512,512]{1,0:T(8,128)}, u32[]{:S(2)}) copy-start(f32[512,512]{1,0:T(8,128)} %param.6) | copy-start | bytes 3145732
  7.2 0.9 copy-start.4
  7.2 183.1 %all-gather.2.cloned.1.call-start = ((), (), s32[]{:S(2)}) async-start(), calls=%async_computation.3 | async-start | bytes 6340608 | tf_op jit(solution)/shard_map/all_gather | solution.py:27
  7.2 15.9 %copy-start.5 = (s32[1,1,192,1]{2,3,1,0:T(1,128)S(1)}, s32[1,1,192,1]{2,3,1,0:T(1,128)}, u32[]{:S(2)}) copy-start(s32[1,1,192,1]{2,3,1,0:T(1,128)} %param.10) | copy-start | bytes 2308
  21.4 2.2 copy-start.6
  21.4 27.7 %copy-start.3 = (f32[1,1,192,1024]{3,2,1,0:T(8,128)S(1)}, f32[1,1,192,1024]{3,2,1,0:T(8,128)}, u32[]{:S(2)}) copy-start(f32[1,1,192,1024]{3,2,1,0:T(8,128)} %param.9) | copy-start | bytes 2359300
  25.7 40.4 %all-to-all-start = ((f32[128,2,1]{1,2,0:T(1,128)}), f32[128,2,1]{1,2,0:T(1,128)S(1)}, u32[]{:S(2)}, u32[]{:S(2)}) async-start(f32[128,2,1]{1,2,0:T(1,128)} %bitcast.10), calls=%async_computation | async-start | bytes 131072 | tf_op jit(solution)/shard_map/all_to_all | solution.py:55
  66.1 130.7 %all-to-all-start.1 = ((f32[128,2,1024]{2,1,0:T(2,128)}), f32[128,2,1024]{2,1,0:T(2,128)S(1)}, u32[]{:S(2)}, u32[]{:S(2)}) async-start(f32[128,2,1024]{2,1,0:T(2,128)} %all_to_all.25), calls=%async_computation.1 | async-start | bytes 2097152 | tf_op jit(solution)/shard_map/all_to_all | solution.py:54
  196.8 1.0 copy-start.2
  197.8 143.3 %all-to-all-start.2 = ((f32[4,3072,128]{1,2,0:T(8,128)}), f32[4,3072,128]{1,2,0:T(8,128)}, u32[]{:S(2)}, u32[]{:S(2)}) async-start(f32[4,3072,128]{1,2,0:T(8,128)} %copy.14), calls=%async_computation.2 | async-start | bytes 12582912 | tf_op jit(solution)/shard_map/all_to_all | solution.py:29
  203.7 2.9 copy-start.1
Sparse Core Ops, SparseCore 0:
  23.3 166.9 all-gather.1
where the time goes:
time: 356 us; the launch traced here: 355 us
  waiting for transfers between devices  254 us (71%)
  starting transfers between devices  35.7 us (10%)
  local copies, waits for them, and re-layouts  16.6 us (5%)
  between operations  14.2 us (4%)
  blocking collectives  13.3 us (4%)
  other arithmetic  12.8 us (4%)
  matrix products  8.63 us (2%)
    all_to_all x1, waiting for transfers between devices, per_device(): lax.all_to_all(split_rows, 'col', split_axis=0, concat_axis=2, tiled=True)  123 us
    all_gather x1, waiting for transfers between devices, per_device(): column_all = lax.all_gather(own_block, 'row', axis=0, tiled=True)  117 us
    all_to_all x1, starting transfers between devices, per_device(): lax.all_to_all(send_ids, 'row', split_axis=0, concat_axis=0, tiled=True)  23.4 us
    all_to_all x1, waiting for transfers between devices, per_device(): lax.all_to_all(send_ids, 'row', split_axis=0, concat_axis=0, tiled=True)  13.9 us
    all_gather x1, blocking collectives, per_device(): panel_whole = lax.all_gather(panel, 'col', axis=1, tiled=True)  13.3 us
    scatter-add x1, other arithmetic, per_device(): blocked.at[landing // tile_cols, :, landing % tile_cols, :]  11.5 us
    dot_general x1, matrix products, per_device(): lax.dot_general(own_full, partner, contract_last, precision=lax.Precision...  7.5 us
  transfers between devices with their start and end apart: 4, of which 3 were waited for; matrix products, arithmetic and copies ran while one was open for 7% of the time, Pallas kernels for 0%

commit v1 on v0

--- a/solution.py
+++ b/solution.py
@@ -6,6 +6,13 @@
 TILE_ROWS = 8
 TILE_COLS = 128
 CAP = 2
+
+
+def all_by_exchange(x, name, dim):
+    size = lax.axis_size(name)
+    blocks = jnp.stack([x for _ in range(size)])
+    blocks = lax.all_to_all(blocks, name, split_axis=0, concat_axis=0)
+    return jnp.concatenate(blocks, axis=dim)
 
 
 def per_device(diag_inverse, panel, trailing, agg_vals, agg_dest, agg_tile):
@@ -24,7 +31,7 @@
         preferred_element_type=jnp.float32,
     )
     own_block = lax.dynamic_slice_in_dim(own_full, col_index * part_width, part_width, 1)
-    column_all = lax.all_gather(own_block, "row", axis=0, tiled=True)
+    column_all = all_by_exchange(own_block, "row", 0)
     split_rows = column_all.reshape(col_devices, local_cols, part_width)
     swapped = lax.all_to_all(split_rows, "col", split_axis=0, concat_axis=2, tiled=True)
     partner = swapped.reshape(local_cols, panel_width)

time: 356 us -> 561 us (1.58)
  blocking collectives: 13.3 us -> 351 us
  waiting for transfers between devices: 254 us -> 136 us
  between operations: 14.2 us -> 0.89 us
    all_to_all x0 -> x1, blocking collectives: none -> 296 us  [all_by_exchange(): blocks = lax.all_to_all(blocks, name, split_axis=0, concat_axis=0)]
    all_gather x1 -> x0, waiting for transfers between devices: 117 us -> none  [per_device(): column_all = lax.all_gather(own_block, 'row', axis=0, tiled=True)]
    all_gather x1, blocking collectives: 13.3 us -> 55.4 us  [per_device(): panel_whole = lax.all_gather(panel, 'col', axis=1, tiled=True)]
    all_to_all x0 -> x1, local copies, waits for them, and re-layouts: none -> 6.53 us  [per_device(): lax.all_to_all(split_rows, 'col', split_axis=0, concat_axis=2, tiled=True)]
    reshape x1 -> x0, local copies, waits for them, and re-layouts: 6.52 us -> none  [per_device(): split_rows = column_all.reshape(col_devices, local_cols, part_width)]
  transfers between devices with their start and end apart: 4 -> 3, of which waited for: 3 -> 2; matrix products, arithmetic and copies ran while one was open for 7% -> 3% of each run, Pallas kernels for 0% -> 0%
where the time goes in v1:
time: 561 us; the launch traced here: 560 us
  blocking collectives  351 us (63%)
  waiting for transfers between devices  136 us (24%)
  starting transfers between devices  35.1 us (6%)
  local copies, waits for them, and re-layouts  15.9 us (3%)
  other arithmetic  12.8 us (2%)
  matrix products  8.63 us (2%)
    all_to_all x1, blocking collectives, all_by_exchange(): blocks = lax.all_to_all(blocks, name, split_axis=0, concat_axis=0)  296 us
    all_to_all x1, waiting for transfers between devices, per_device(): lax.all_to_all(split_rows, 'col', split_axis=0, concat_axis=2, tiled=True)  122 us
    all_gather x1, blocking collectives, per_device(): panel_whole = lax.all_gather(panel, 'col', axis=1, tiled=True)  55.4 us
    all_to_all x1, starting transfers between devices, per_device(): lax.all_to_all(send_ids, 'row', split_axis=0, concat_axis=0, tiled=True)  23 us
    all_to_all x1, waiting for transfers between devices, per_device(): lax.all_to_all(send_ids, 'row', split_axis=0, concat_axis=0, tiled=True)  13.8 us
    scatter-add x1, other arithmetic, per_device(): blocked.at[landing // tile_cols, :, landing % tile_cols, :]  11.5 us
  transfers between devices with their start and end apart: 3, of which 2 were waited for; matrix products, arithmetic and copies ran while one was open for 3% of the time, Pallas kernels for 0%

profile of v1, /device:TPU:1, one launch (start us, length us, event | category | flops | bytes accessed | tf_op | source)
XLA Modules:
  0.0 560.3 jit_solution(2083762842664101898)
XLA Ops:
  0.6 0.0 copy-start
  0.6 0.0 copy-start.6
  0.7 0.0 copy-start.7
  0.7 0.0 copy-start.3
  0.7 0.7 copy-done.6
  1.4 0.1 iota_compare_fusion
  1.5 0.1 fusion.3
  1.8 0.2 fusion.6
  2.0 0.0 copy-done.7
  2.0 1.2 scatter_custom_fusion
  3.2 0.8 all_to_all.26
  3.9 23.0 %all-to-all-start = ((f32[128,2,1]{1,2,0:T(1,128)}), f32[128,2,1]{1,2,0:T(1,128)S(1)}, u32[]{:S(2)}, u32[]{:S(2)}) async-start(f32[128,2,1]{1,2,0:T(1,128)} %bitcast.10), calls=%async_computation | async-start | bytes 131072 | tf_op jit(solution)/shard_map/all_to_all | solution.py:62
  27.0 0.0 copy-done.3
  27.0 1.5 scatter_custom_fusion.1
  28.5 1.6 all_to_all.28
  30.1 0.0 copy-start.5
  30.1 13.8 %all-to-all-done = f32[128,2,1]{1,2,0:T(1,128)S(1)} async-done(((f32[128,2,1]{1,2,0:T(1,128)}), f32[128,2,1]{1,2,0:T(1,128)S(1)}, u32[]{:S(2)}, u32[]{:S(2)}) %all-to-all-start) | async-done | bytes 1056 | tf_op jit(solution)/shard_map/all_to_all | solution.py:62
  43.9 6.7 %all-to-all-start.1 = ((f32[128,2,1024]{2,1,0:T(2,128)}), f32[128,2,1024]{2,1,0:T(2,128)S(1)}, u32[]{:S(2)}, u32[]{:S(2)}) async-start(f32[128,2,1024]{2,1,0:T(2,128)} %all_to_all.28), calls=%async_computation.1 | async-start | bytes 2097152 | tf_op jit(solution)/shard_map/all_to_all | solution.py:61
  50.6 0.0 copy-done.5
  50.7 55.4 %all_gather.3 = f32[96,512]{1,0:T(8,128)S(1)} all-gather(f32[96,128]{1,0:T(8,128)S(1)} %copy-done.5), channel_id=1, replica_groups=mesh['row'=128,'col'=4] {'col'}, dimensions={1}, use_global_device_ids=true | all-gather | bytes 245760 | tf_op jit(solution)/shard_map/all_gather | solution.py:26
  106.0 0.0 copy-done
  106.0 1.1 fusion.10
  107.2 0.0 copy-start.4
  107.2 0.0 all-to-all-done.1
  107.2 0.0 copy-start.2
  107.2 0.8 stack.2
  108.0 0.0 copy-done.4
  108.0 0.2 copy-done.2
  108.2 295.8 %all_to_all.38 = f32[128,96,128]{2,1,0:T(8,128)} all-to-all(f32[128,96,128]{2,1,0:T(8,128)S(1)} %stack.2), channel_id=1, replica_groups=mesh['row'=128,'col'=4] {'row'}, dimensions={0} | all-to-all | bytes 12582912 | tf_op jit(solution)/shard_map/all_to_all | solution.py:14
  404.0 5.4 all-to-all-start.3
  409.4 0.5 divide_reduce_fusion
  410.0 0.0 copy-start.1
  410.0 0.1 rem.30
  410.1 0.1 div.17
  410.3 0.3 compare_reduce_fusion
  410.6 0.1 ne.52
  410.7 2.1 reshape.172
  412.8 0.0 copy-done.1
  412.8 11.5 %scatter_fusion = f32[12,8,24,128]{3,1,2,0:T(8,128)S(1)} fusion(f32[12,8,24,128]{3,1,2,0:T(8,128)S(1)} %bitcast.37, s32[256]{0:T(256)S(1)} %bitcast.36, f32[256,8,128]{2,1,0:T(8,128)S(1)} %reshape.172), kind=kCustom, calls=%fused_computation.2 | custom fusion | flops 262144 | bytes 3147776 | tf_op jit(solution)/shard_map/scatter-add | solution.py:66
  424.3 122.0 %all-to-all-done.3 = f32[4,3072,128]{2,1,0:T(8,128)} async-done(((f32[4,3072,128]{2,1,0:T(8,128)}), f32[4,3072,128]{2,1,0:T(8,128)}, u32[]{:S(2)}, u32[]{:S(2)}) %all-to-all-start.3) | async-done | bytes 6291488 | tf_op jit(solution)/shard_map/all_to_all | solution.py:36
  546.3 6.5 %copy.16 = f32[1,3072,4,128]{1,3,2,0:T(8,128)} copy(f32[1,3072,4,128]{3,1,2,0:T(8,128)} %bitcast.16) | data formatting | bytes 12582912 | tf_op jit(solution)/shard_map/all_to_all | solution.py:36
  552.8 7.5 %convolution_subtract_fusion = f32[96,3072]{1,0:T(8,128)} fusion(f32[96,512]{1,0:T(8,128)S(1)} %fusion.10, f32[3072,512]{0,1:T(8,128)} %bitcast.35, f32[12,8,24,128]{3,1,2,0:T(8,128)S(1)} %scatter_fusion), kind=kOutput, calls=%fused_computation.3 | convolution fusion | flops 1812234240 | bytes 8847360 | tf_op jit(solution)/shard_map/dot_general | solution.py:70
  (11 shorter events, 0.1 us)
Async XLA Ops:
  0.6 105.4 %copy-start = (f32[512,512]{1,0:T(8,128)S(1)}, f32[512,512]{1,0:T(8,128)}, u32[]{:S(2)}) copy-start(f32[512,512]{1,0:T(8,128)} %param.6) | copy-start | bytes 3145732
  0.6 0.8 copy-start.6
  0.7 1.3 copy-start.7
  0.7 26.3 %copy-start.3 = (f32[1,1,192,1024]{3,2,1,0:T(8,128)S(1)}, f32[1,1,192,1024]{3,2,1,0:T(8,128)}, u32[]{:S(2)}) copy-start(f32[1,1,192,1024]{3,2,1,0:T(8,128)} %param.9) | copy-start | bytes 2359300
  3.9 40.0 %all-to-all-start = ((f32[128,2,1]{1,2,0:T(1,128)}), f32[128,2,1]{1,2,0:T(1,128)S(1)}, u32[]{:S(2)}, u32[]{:S(2)}) async-start(f32[128,2,1]{1,2,0:T(1,128)} %bitcast.10), calls=%async_computation | async-start | bytes 131072 | tf_op jit(solution)/shard_map/all_to_all | solution.py:62
  30.1 20.5 %copy-start.5 = (f32[96,128]{1,0:T(8,128)S(1)}, f32[96,128]{1,0:T(8,128)}, u32[]{:S(2)}) copy-start(f32[96,128]{1,0:T(8,128)} %param.7) | copy-start | bytes 147460
  43.9 63.3 %all-to-all-start.1 = ((f32[128,2,1024]{2,1,0:T(2,128)}), f32[128,2,1024]{2,1,0:T(2,128)S(1)}, u32[]{:S(2)}, u32[]{:S(2)}) async-start(f32[128,2,1024]{2,1,0:T(2,128)} %all_to_all.28), calls=%async_computation.1 | async-start | bytes 2097152 | tf_op jit(solution)/shard_map/all_to_all | solution.py:61
  107.2 0.8 copy-start.4
  107.2 1.0 copy-start.2
  404.0 142.3 %all-to-all-start.3 = ((f32[4,3072,128]{2,1,0:T(8,128)}), f32[4,3072,128]{2,1,0:T(8,128)}, u32[]{:S(2)}, u32[]{:S(2)}) async-start(f32[4,3072,128]{2,1,0:T(8,128)} %bitcast.34), calls=%async_computation.3 | async-start | bytes 12582912 | tf_op jit(solution)/shard_map/all_to_all | solution.py:36
  410.0 2.9 copy-start.1
